TPU v7x, 512 devices: a whole 4x8x8 slice. The times are simulated.
512 devices in a mesh: dev: 32 (over y_hi, z), ha: 2 (over y_lo), col: 8 (over x, core).
Axes of the slice: x: 4, y: 8 (y_hi: 4, y_lo: 2; y = y_hi * 2 + y_lo), z: 8, core: 2. Of those that a mesh axis runs over, the one named last changes fastest.
Arguments:
- features: bfloat16 [128, 128, 32, 128], P('col', 'dev', 'ha'), may hold values from -6 to 6
- kernel: bfloat16 [3, 3, 3, 128, 128], P(None, None, None, 'col'), may hold values from -0.109375 to 0.109375
- channel_bias: float32 [128], P('col'), may hold values from -3 to 3
Outputs:
- activated: bfloat16 [128, 128, 32, 128], P('col', 'dev', 'ha')
All inputs are finite; a program needn't handle non-finite values.
Results may differ from a plain program's by a relative error of at most 0.005.
Values may be sent and summed in bfloat16 or wider, within the bound.
A program may use at most 64 MiB of HBM per device.

v0:
```python
import jax
import jax.numpy as jnp
from jax import lax
from jax.sharding import PartitionSpec as P


def with_halo(x, sides, width):
    for axis, dim in sides:
        devices, length = (lax.axis_size(axis), x.shape[dim])
        up = [(i, (i + 1) % devices) for i in range(devices - 1)]
        down = [(j, i) for i, j in up]
        last = lax.slice_in_dim(x, length - width, length, axis=dim)
        first = lax.slice_in_dim(x, 0, width, axis=dim)
        before = lax.ppermute(last, axis, up)
        after = lax.ppermute(first, axis, down)
        x = jnp.concatenate([before, x, after], axis=dim)
    return x


def convolve(padded, weights):
    depth_pad = padded.shape[1]
    height_pad = padded.shape[2]
    width_cells = padded.shape[3]
    outer = weights.shape[3]
    depth_cells = depth_pad - 2
    height_cells = height_pad - 2
    partial_sums = [
        jnp.zeros((outer, depth_cells, height_cells, width_cells), jnp.float32)
        for col_tap in range(3)
    ]
    for depth_tap in range(3):
        planes = padded[:, depth_tap : depth_tap + depth_cells]
        tap_out = lax.dot_general(
            weights[depth_tap], planes, (((3,), (0,)), ((), ())), preferred_element_type=jnp.float32
        )
        for row_tap in range(3):
            for col_tap in range(3):
                partial_sums[col_tap] = (
                    partial_sums[col_tap]
                    + tap_out[row_tap, col_tap, :, :, row_tap : row_tap + height_cells, :]
                )
    zero_column = jnp.zeros((outer, depth_cells, height_cells, 1), jnp.float32)
    from_left = jnp.concatenate([zero_column, partial_sums[0][..., :-1]], axis=3)
    from_right = jnp.concatenate([partial_sums[2][..., 1:], zero_column], axis=3)
    return partial_sums[1] + from_left + from_right


def finish(summed, offsets):
    summed = summed + offsets[:, None, None, None]
    return jnp.where(summed >= 0, summed, 0.3 * summed).astype(jnp.bfloat16)


def per_device(features, kernel, channel_bias):
    padded = with_halo(features, (("dev", 1), ("ha", 2)), 1)
    gathered = lax.all_gather(padded, "col", axis=0, tiled=True)
    return finish(convolve(gathered, kernel), channel_bias)


def solution(mesh):
    in_specs = (P("col", "dev", "ha", None), P(None, None, None, "col", None), P("col"))
    out_specs = P("col", "dev", "ha", None)
    return jax.shard_map(
        per_device, mesh=mesh, in_specs=in_specs, out_specs=out_specs, check_vma=False
    )
```

profile of v0, /device:TPU:1, one launch (start us, length us, event | category | flops | bytes accessed | tf_op | source)
XLA Modules:
  0.0 85.2 jit_solution(9481461446292273636)
XLA Ops:
  6.5 0.0 all-gather.2.cloned.1.call-start
  6.5 0.9 %fusion.24 = (bf16[16,1,16,128]{3,2,1,0:T(8,128)(2,1)S(1)}, bf16[16,1,16,128]{3,2,1,0:T(8,128)(2,1)S(1)}) fusion(bf16[16,4,16,128]{3,2,1,0:T(8,128)(2,1)} %param.3), kind=kLoop, calls=%fused_computation.61 | loop fusion | bytes 262144 | tf_op jit(solution)/shard_map/slice | solution.py:13
  7.5 4.8 %collective-permute-start = (bf16[16,1,16,128]{3,0,2,1:T(8,128)(2,1)S(1)}, bf16[16,1,16,128]{3,0,2,1:T(8,128)(2,1)S(1)}, u32[]{:S(2)}, u32[]{:S(2)}) collective-permute-start(bf16[16,1,16,128]{3,0,2,1:T(8,128)(2,1)S(1)} %copy.37), channel_id=1, source_target_pairs={{0,16},{16,32},{32,48},{48,64},{64,80},{80,96},{96,112},{112,128},... | collective-permute-start | bytes 196616 | tf_op jit(solution)/shard_map/ppermute | solution.py:14
  12.3 1.3 %collective-permute-start.1 = (bf16[16,1,16,128]{3,0,2,1:T(8,128)(2,1)S(1)}, bf16[16,1,16,128]{3,0,2,1:T(8,128)(2,1)S(1)}, u32[]{:S(2)}, u32[]{:S(2)}) collective-permute-start(bf16[16,1,16,128]{3,0,2,1:T(8,128)(2,1)S(1)} %copy.38), channel_id=1, source_target_pairs={{16,0},{32,16},{48,32},{64,48},{80,64},{96,80},{112,96},{128,112},... | collective-permute-start | bytes 196616 | tf_op jit(solution)/shard_map/ppermute | solution.py:15
  13.6 0.0 collective-permute-done
  13.6 1.1 %constant_dynamic-update-slice_fusion.1 = bf16[16,6,16,128]{3,0,2,1:T(8,128)(2,1)S(1)} fusion(bf16[16,6,16,128]{3,0,2,1:T(8,128)(2,1)S(1)} %constant_dynamic-update-slice_fusion.2, bf16[16,4,16,128]{3,2,1,0:T(8,128)(2,1)} %param.3), kind=kLoop, calls=%fused_computation.58 | loop fusion | bytes 524288
  14.8 3.2 %collective-permute-done.1 = bf16[16,1,16,128]{3,0,2,1:T(8,128)(2,1)S(1)} collective-permute-done((bf16[16,1,16,128]{3,0,2,1:T(8,128)(2,1)S(1)}, bf16[16,1,16,128]{3,0,2,1:T(8,128)(2,1)S(1)}, u32[]{:S(2)}, u32[]{:S(2)}) %collective-permute-start.1) | collective-permute-done | bytes 65568 | tf_op jit(solution)/shard_map/ppermute | solution.py:15
  18.0 3.2 %collective-permute-start.2 = (bf16[16,6,1,128]{3,0,2,1:T(8,128)(2,1)S(1)}, bf16[16,6,1,128]{3,0,2,1:T(8,128)(2,1)S(1)}, u32[]{:S(2)}, u32[]{:S(2)}) collective-permute-start(bf16[16,6,1,128]{3,0,2,1:T(8,128)(2,1)S(1)} %get-tuple-element.5), channel_id=1, source_target_pairs={{0,8},{1,9},{2,10},{3,11},{4,12},{5,13},{6,14},{7,15},{16,24},{17,... | collective-permute-start | bytes 73736 | tf_op jit(solution)/shard_map/ppermute | solution.py:14
  21.2 1.3 %collective-permute-start.3 = (bf16[16,6,1,128]{3,0,2,1:T(8,128)(2,1)S(1)}, bf16[16,6,1,128]{3,0,2,1:T(8,128)(2,1)S(1)}, u32[]{:S(2)}, u32[]{:S(2)}) collective-permute-start(bf16[16,6,1,128]{3,0,2,1:T(8,128)(2,1)S(1)} %get-tuple-element.6), channel_id=1, source_target_pairs={{8,0},{9,1},{10,2},{11,3},{12,4},{13,5},{14,6},{15,7},{24,16},{25,... | collective-permute-start | bytes 73736 | tf_op jit(solution)/shard_map/ppermute | solution.py:15
  22.5 0.0 collective-permute-done.2
  22.5 3.3 %collective-permute-done.3 = bf16[16,6,1,128]{3,0,2,1:T(8,128)(2,1)S(1)} collective-permute-done((bf16[16,6,1,128]{3,0,2,1:T(8,128)(2,1)S(1)}, bf16[16,6,1,128]{3,0,2,1:T(8,128)(2,1)S(1)}, u32[]{:S(2)}, u32[]{:S(2)}) %collective-permute-start.3) | collective-permute-done | bytes 24608 | tf_op jit(solution)/shard_map/ppermute | solution.py:15
  25.8 0.8 pad_maximum_fusion
  26.6 0.0 all-gather.2.cloned.1.call-update
  26.7 0.0 copy-start.1
  26.7 45.2 %all-gather.2.cloned.1.call-done = bf16[128,6,18,128]{3,0,2,1:T(8,128)(2,1)} async-done(((bf16[16,6,18,128]{3,0,2,1:T(8,128)(2,1)}), bf16[128,6,18,128]{3,0,2,1:T(8,128)(2,1)}) %all-gather.2.cloned.1.call-update) | async-done | bytes 3538960 | tf_op jit(solution)/shard_map/all_gather | solution.py:55
  71.9 0.0 copy-start
  71.9 2.7 %convolution_bitcast_fusion = f32[3,3,16,4,18,128]{5,2,4,3,1,0:T(8,128)S(1)} fusion(bf16[128,6,18,128]{3,0,2,1:T(8,128)(2,1)} %all-gather.2.cloned.1.call-done, bf16[3,3,3,16,128]{4,3,2,1,0:T(8,128)(2,1)} %param.4), kind=kOutput, calls=%fused_computation | convolution fusion | flops 339738624 | bytes 7704576 | tf_op jit(solution)/shard_map/dot_general | solution.py:33
  74.6 0.0 copy-done.1
  74.6 0.1 copy-done
  74.6 0.8 convolution_bitcast_fusion.1
  75.5 0.8 convolution_bitcast_fusion.2
  76.3 0.0 copy-start.2
  76.3 0.3 fusion.2
  76.7 0.3 fusion.8
  77.0 0.2 slice.191
  77.2 0.0 copy-done.2
  77.2 0.4 fusion
  77.6 0.8 copy.21
  (5 shorter events, 0.1 us)
Async XLA Ops:
  6.5 65.4 %all-gather.2.cloned.1.call-start = ((), (), s32[]{:S(2)}) async-start(), calls=%async_computation | async-start | bytes 3981312 | tf_op jit(solution)/shard_map/all_gather | solution.py:55
  7.5 6.2 %collective-permute-start = (bf16[16,1,16,128]{3,0,2,1:T(8,128)(2,1)S(1)}, bf16[16,1,16,128]{3,0,2,1:T(8,128)(2,1)S(1)}, u32[]{:S(2)}, u32[]{:S(2)}) collective-permute-start(bf16[16,1,16,128]{3,0,2,1:T(8,128)(2,1)S(1)} %copy.37), channel_id=1, source_target_pairs={{0,16},{16,32},{32,48},{48,64},{64,80},{80,96},{96,112},{112,128},... | collective-permute-start | bytes 196616 | tf_op jit(solution)/shard_map/ppermute | solution.py:14
  12.3 5.6 %collective-permute-start.1 = (bf16[16,1,16,128]{3,0,2,1:T(8,128)(2,1)S(1)}, bf16[16,1,16,128]{3,0,2,1:T(8,128)(2,1)S(1)}, u32[]{:S(2)}, u32[]{:S(2)}) collective-permute-start(bf16[16,1,16,128]{3,0,2,1:T(8,128)(2,1)S(1)} %copy.38), channel_id=1, source_target_pairs={{16,0},{32,16},{48,32},{64,48},{80,64},{96,80},{112,96},{128,112},... | collective-permute-start | bytes 196616 | tf_op jit(solution)/shard_map/ppermute | solution.py:15
  18.0 4.5 %collective-permute-start.2 = (bf16[16,6,1,128]{3,0,2,1:T(8,128)(2,1)S(1)}, bf16[16,6,1,128]{3,0,2,1:T(8,128)(2,1)S(1)}, u32[]{:S(2)}, u32[]{:S(2)}) collective-permute-start(bf16[16,6,1,128]{3,0,2,1:T(8,128)(2,1)S(1)} %get-tuple-element.5), channel_id=1, source_target_pairs={{0,8},{1,9},{2,10},{3,11},{4,12},{5,13},{6,14},{7,15},{16,24},{17,... | collective-permute-start | bytes 73736 | tf_op jit(solution)/shard_map/ppermute | solution.py:14
  21.2 4.6 %collective-permute-start.3 = (bf16[16,6,1,128]{3,0,2,1:T(8,128)(2,1)S(1)}, bf16[16,6,1,128]{3,0,2,1:T(8,128)(2,1)S(1)}, u32[]{:S(2)}, u32[]{:S(2)}) collective-permute-start(bf16[16,6,1,128]{3,0,2,1:T(8,128)(2,1)S(1)} %get-tuple-element.6), channel_id=1, source_target_pairs={{8,0},{9,1},{10,2},{11,3},{12,4},{13,5},{14,6},{15,7},{24,16},{25,... | collective-permute-start | bytes 73736 | tf_op jit(solution)/shard_map/ppermute | solution.py:15
  26.7 47.9 %copy-start.1 = (bf16[3,3,3,16,128]{4,3,2,1,0:T(8,128)(2,1)S(1)}, bf16[3,3,3,16,128]{4,3,2,1,0:T(8,128)(2,1)}, u32[]{:S(2)}) copy-start(bf16[3,3,3,16,128]{4,3,2,1,0:T(8,128)(2,1)} %param.4) | copy-start | bytes 331780
  71.9 2.7 %copy-start = (bf16[128,6,18,128]{3,0,2,1:T(8,128)(2,1)S(1)}, bf16[128,6,18,128]{3,0,2,1:T(8,128)(2,1)}, u32[]{:S(2)}) copy-start(bf16[128,6,18,128]{3,0,2,1:T(8,128)(2,1)} %all-gather.2.cloned.1.call-done) | copy-start | bytes 10616836
  76.3 0.8 copy-start.2
Sparse Core Ops, SparseCore 0:
  26.8 45.0 all-gather.1
where the time goes:
time: 85.4 us; the launch traced here: 85.2 us
  waiting for transfers between devices  51.7 us (61%)
  between operations  13.5 us (16%)
  starting transfers between devices  10.6 us (12%)
  matrix products  4.34 us (5%)
  local copies, waits for them, and re-layouts  3.13 us (4%)
  other arithmetic  1.86 us (2%)
    all_gather x1, waiting for transfers between devices, per_device(): gathered = lax.all_gather(padded, 'col', axis=0, tiled=True)  45.2 us
    ppermute x2, starting transfers between devices, with_halo(): before = lax.ppermute(last, axis, up)  8.02 us
    ppermute x2, waiting for transfers between devices, with_halo(): after = lax.ppermute(first, axis, down)  6.47 us
    dot_general x3, matrix products, convolve(): lax.dot_general(weights[depth_tap], planes, (((3,), (0,)), ((), ())), pre...  4.34 us
    ppermute x2, starting transfers between devices, with_halo(): after = lax.ppermute(first, axis, down)  2.58 us
  transfers between devices with their start and end apart: 5, of which 3 were waited for; matrix products, arithmetic and copies ran while one was open for 1% of the time, Pallas kernels for 0%

commit v1 on v0

--- a/solution.py
+++ b/solution.py
@@ -2,6 +2,7 @@
 import jax.numpy as jnp
 from jax import lax
 from jax.sharding import PartitionSpec as P
+from jax.lax import all_to_all, axis_size
 
 
 def with_halo(x, sides, width):
@@ -52,7 +53,9 @@
 
 def per_device(features, kernel, channel_bias):
     padded = with_halo(features, (("dev", 1), ("ha", 2)), 1)
-    gathered = lax.all_gather(padded, "col", axis=0, tiled=True)
+    gathered = jnp.concatenate(
+        all_to_all(jnp.stack(tuple((padded for _ in range(axis_size("col"))))), "col", 0, 0), axis=0
+    )
     return finish(convolve(gathered, kernel), channel_bias)
 
 

time: 85.4 us -> 80.2 us (0.939)
  the two profiles are of different devices: /device:TPU:1 before, /device:TPU:48 now
where the time goes in v1:
time: 80.2 us; the launch traced here: 79.9 us
  blocking collectives  46.8 us (58%)
  starting transfers between devices  17.9 us (22%)
  waiting for transfers between devices  6.42 us (8%)
  local copies, waits for them, and re-layouts  4.82 us (6%)
  matrix products  2.51 us (3%)
  other arithmetic  1.37 us (2%)
    all_to_all x1, blocking collectives, per_device(): all_to_all(jnp.stack(tuple((padded for _ in range(axis_size('col'))))), '...  46.8 us
    ppermute x2, starting transfers between devices, with_halo(): after = lax.ppermute(first, axis, down)  11.5 us
    ppermute x2, starting transfers between devices, with_halo(): before = lax.ppermute(last, axis, up)  6.44 us
    ppermute x2, waiting for transfers between devices, with_halo(): after = lax.ppermute(first, axis, down)  4.43 us
    dot_general x3, matrix products, convolve(): lax.dot_general(weights[depth_tap], planes, (((3,), (0,)), ((), ())), pre...  2.51 us
    ppermute x2, waiting for transfers between devices, with_halo(): before = lax.ppermute(last, axis, up)  1.99 us
  transfers between devices with their start and end apart: 4, of which 4 were waited for; matrix products, arithmetic and copies ran while one was open for 1% of the time, Pallas kernels for 0%

profile of v1, /device:TPU:48, one launch (start us, length us, event | category | flops | bytes accessed | tf_op | source)
XLA Modules:
  0.0 79.9 jit_solution(2465866957395272365)
XLA Ops:
  0.0 0.9 %fusion.24 = (bf16[16,1,16,128]{3,2,1,0:T(8,128)(2,1)S(1)}, bf16[16,1,16,128]{3,2,1,0:T(8,128)(2,1)S(1)}) fusion(bf16[16,4,16,128]{3,2,1,0:T(8,128)(2,1)} %param.3), kind=kLoop, calls=%fused_computation.61 | loop fusion | bytes 262144 | tf_op jit(solution)/shard_map/slice | solution.py:14
  0.9 4.3 %collective-permute-start = (bf16[16,1,16,128]{3,2,1,0:T(8,128)(2,1)S(1)}, bf16[16,1,16,128]{3,2,1,0:T(8,128)(2,1)S(1)}, u32[]{:S(2)}, u32[]{:S(2)}) collective-permute-start(bf16[16,1,16,128]{3,2,1,0:T(8,128)(2,1)S(1)} %get-tuple-element.8), channel_id=1, source_target_pairs={{0,16},{16,32},{32,48},{48,64},{64,80},{80,96},{96,112},{112,128},... | collective-permute-start | bytes 196616 | tf_op jit(solution)/shard_map/ppermute | solution.py:15
  5.2 10.2 %collective-permute-start.1 = (bf16[16,1,16,128]{3,2,1,0:T(8,128)(2,1)S(1)}, bf16[16,1,16,128]{3,2,1,0:T(8,128)(2,1)S(1)}, u32[]{:S(2)}, u32[]{:S(2)}) collective-permute-start(bf16[16,1,16,128]{3,2,1,0:T(8,128)(2,1)S(1)} %get-tuple-element.7), channel_id=1, source_target_pairs={{16,0},{32,16},{48,32},{64,48},{80,64},{96,80},{112,96},{128,112},... | collective-permute-start | bytes 196616 | tf_op jit(solution)/shard_map/ppermute | solution.py:16
  15.3 1.6 %collective-permute-done = bf16[16,1,16,128]{3,2,1,0:T(8,128)(2,1)S(1)} collective-permute-done((bf16[16,1,16,128]{3,2,1,0:T(8,128)(2,1)S(1)}, bf16[16,1,16,128]{3,2,1,0:T(8,128)(2,1)S(1)}, u32[]{:S(2)}, u32[]{:S(2)}) %collective-permute-start) | collective-permute-done | bytes 65568 | tf_op jit(solution)/shard_map/ppermute | solution.py:15
  16.9 1.0 %constant_dynamic-update-slice_fusion.1 = bf16[16,6,16,128]{3,2,1,0:T(8,128)(2,1)S(1)} fusion(bf16[16,6,16,128]{3,2,1,0:T(8,128)(2,1)S(1)} %constant_dynamic-update-slice_fusion.2, bf16[16,4,16,128]{3,2,1,0:T(8,128)(2,1)} %param.3), kind=kLoop, calls=%fused_computation.58 | loop fusion | bytes 524288
  17.9 0.2 collective-permute-done.1
  18.1 0.1 fusion.23
  18.2 2.2 %collective-permute-start.2 = (bf16[16,6,1,128]{3,2,1,0:T(2,128)(2,1)S(1)}, bf16[16,6,1,128]{3,2,1,0:T(2,128)(2,1)S(1)}, u32[]{:S(2)}, u32[]{:S(2)}) collective-permute-start(bf16[16,6,1,128]{3,2,1,0:T(2,128)(2,1)S(1)} %get-tuple-element.5), channel_id=1, source_target_pairs={{0,8},{1,9},{2,10},{3,11},{4,12},{5,13},{6,14},{7,15},{16,24},{17,... | collective-permute-start | bytes 73736 | tf_op jit(solution)/shard_map/ppermute | solution.py:15
  20.3 1.3 %collective-permute-start.3 = (bf16[16,6,1,128]{3,2,1,0:T(2,128)(2,1)S(1)}, bf16[16,6,1,128]{3,2,1,0:T(2,128)(2,1)S(1)}, u32[]{:S(2)}, u32[]{:S(2)}) collective-permute-start(bf16[16,6,1,128]{3,2,1,0:T(2,128)(2,1)S(1)} %get-tuple-element.6), channel_id=1, source_target_pairs={{8,0},{9,1},{10,2},{11,3},{12,4},{13,5},{14,6},{15,7},{24,16},{25,... | collective-permute-start | bytes 73736 | tf_op jit(solution)/shard_map/ppermute | solution.py:16
  21.6 0.4 collective-permute-done.2
  22.1 4.3 %collective-permute-done.3 = bf16[16,6,1,128]{3,2,1,0:T(2,128)(2,1)S(1)} collective-permute-done((bf16[16,6,1,128]{3,2,1,0:T(2,128)(2,1)S(1)}, bf16[16,6,1,128]{3,2,1,0:T(2,128)(2,1)S(1)}, u32[]{:S(2)}, u32[]{:S(2)}) %collective-permute-start.3) | collective-permute-done | bytes 24608 | tf_op jit(solution)/shard_map/ppermute | solution.py:16
  26.3 0.3 pad_maximum_fusion
  26.7 0.1 copy.20
  26.8 0.6 stack.2
  27.4 46.8 %all_to_all.5 = bf16[8,16,6,18,128]{4,1,3,2,0:T(8,128)(2,1)S(1)} all-to-all(bf16[8,16,6,18,128]{4,1,3,2,0:T(8,128)(2,1)S(1)} %stack.2), channel_id=1, replica_groups=mesh['dev'=32,'ha'=2,'col'=8] {'col'}, dimensions={0} | all-to-all | bytes 7077888 | tf_op jit(solution)/shard_map/all_to_all | solution.py:57
  74.1 0.0 copy-start
  74.1 1.0 %copy.21 = bf16[8,16,6,18,128]{4,1,0,3,2:T(8,128)(2,1)S(1)} copy(bf16[8,16,6,18,128]{4,1,3,2,0:T(8,128)(2,1)S(1)} %all_to_all.5) | data formatting | bytes 7077888 | tf_op jit(solution)/shard_map/all_to_all | solution.py:57
  75.2 0.0 copy-done
  75.2 0.8 %convolution_bitcast_fusion = f32[3,3,16,4,18,128]{5,2,4,3,1,0:T(8,128)S(1)} fusion(bf16[128,6,18,128]{3,0,2,1:T(8,128)(2,1)S(1)} %bitcast.126, bf16[3,3,3,16,128]{4,3,2,1,0:T(8,128)(2,1)S(1)} %copy-done), kind=kOutput, calls=%fused_computation | convolution fusion | flops 339738624 | bytes 7704576 | tf_op jit(solution)/shard_map/dot_general | solution.py:34
  76.0 0.8 %convolution_bitcast_fusion.1 = f32[3,3,16,4,18,128]{5,2,4,3,1,0:T(8,128)S(1)} fusion(bf16[128,6,18,128]{3,0,2,1:T(8,128)(2,1)S(1)} %bitcast.127, bf16[3,3,3,16,128]{4,3,2,1,0:T(8,128)(2,1)S(1)} %copy-done), kind=kOutput, calls=%fused_computation.1 | convolution fusion | flops 339738624 | bytes 7704576 | tf_op jit(solution)/shard_map/dot_general | solution.py:34
  76.9 0.8 %convolution_bitcast_fusion.2 = f32[3,3,16,4,18,128]{5,2,1,0,4,3:T(8,128)S(1)} fusion(bf16[128,6,18,128]{3,0,2,1:T(8,128)(2,1)S(1)} %bitcast.128, bf16[3,3,3,16,128]{4,3,2,1,0:T(8,128)(2,1)S(1)} %copy-done), kind=kOutput, calls=%fused_computation.2 | convolution fusion | flops 339738624 | bytes 7704576 | tf_op jit(solution)/shard_map/dot_general | solution.py:34
  77.7 0.3 fusion.2
  78.1 0.0 copy-start.1
  78.1 0.3 fusion.8
  78.4 0.2 slice.189
  78.6 0.1 copy-done.1
  78.7 0.4 fusion
  79.1 0.8 copy.36
  (2 shorter events, 0.0 us)
Async XLA Ops:
  0.9 16.0 %collective-permute-start = (bf16[16,1,16,128]{3,2,1,0:T(8,128)(2,1)S(1)}, bf16[16,1,16,128]{3,2,1,0:T(8,128)(2,1)S(1)}, u32[]{:S(2)}, u32[]{:S(2)}) collective-permute-start(bf16[16,1,16,128]{3,2,1,0:T(8,128)(2,1)S(1)} %get-tuple-element.8), channel_id=1, source_target_pairs={{0,16},{16,32},{32,48},{48,64},{64,80},{80,96},{96,112},{112,128},... | collective-permute-start | bytes 196616 | tf_op jit(solution)/shard_map/ppermute | solution.py:15
  5.2 12.9 %collective-permute-start.1 = (bf16[16,1,16,128]{3,2,1,0:T(8,128)(2,1)S(1)}, bf16[16,1,16,128]{3,2,1,0:T(8,128)(2,1)S(1)}, u32[]{:S(2)}, u32[]{:S(2)}) collective-permute-start(bf16[16,1,16,128]{3,2,1,0:T(8,128)(2,1)S(1)} %get-tuple-element.7), channel_id=1, source_target_pairs={{16,0},{32,16},{48,32},{64,48},{80,64},{96,80},{112,96},{128,112},... | collective-permute-start | bytes 196616 | tf_op jit(solution)/shard_map/ppermute | solution.py:16
  18.2 3.9 %collective-permute-start.2 = (bf16[16,6,1,128]{3,2,1,0:T(2,128)(2,1)S(1)}, bf16[16,6,1,128]{3,2,1,0:T(2,128)(2,1)S(1)}, u32[]{:S(2)}, u32[]{:S(2)}) collective-permute-start(bf16[16,6,1,128]{3,2,1,0:T(2,128)(2,1)S(1)} %get-tuple-element.5), channel_id=1, source_target_pairs={{0,8},{1,9},{2,10},{3,11},{4,12},{5,13},{6,14},{7,15},{16,24},{17,... | collective-permute-start | bytes 73736 | tf_op jit(solution)/shard_map/ppermute | solution.py:15
  20.3 6.0 %collective-permute-start.3 = (bf16[16,6,1,128]{3,2,1,0:T(2,128)(2,1)S(1)}, bf16[16,6,1,128]{3,2,1,0:T(2,128)(2,1)S(1)}, u32[]{:S(2)}, u32[]{:S(2)}) collective-permute-start(bf16[16,6,1,128]{3,2,1,0:T(2,128)(2,1)S(1)} %get-tuple-element.6), channel_id=1, source_target_pairs={{8,0},{9,1},{10,2},{11,3},{12,4},{13,5},{14,6},{15,7},{24,16},{25,... | collective-permute-start | bytes 73736 | tf_op jit(solution)/shard_map/ppermute | solution.py:16
  74.1 1.1 %copy-start = (bf16[3,3,3,16,128]{4,3,2,1,0:T(8,128)(2,1)S(1)}, bf16[3,3,3,16,128]{4,3,2,1,0:T(8,128)(2,1)}, u32[]{:S(2)}) copy-start(bf16[3,3,3,16,128]{4,3,2,1,0:T(8,128)(2,1)} %param.4) | copy-start | bytes 331780
  78.1 0.7 copy-start.1
